TPU v7x, 256 devices: a whole 4x4x8 slice. The times are simulated.
256 devices in a mesh: dp: 8 (over x, y_lo), fsdp: 16 (over z, core), tensor: 2 (over y_hi).
Axes of the slice: x: 4, y: 4 (y_hi: 2, y_lo: 2; y = y_hi * 2 + y_lo), z: 8, core: 2. Of those that a mesh axis runs over, the one named last changes fastest.
Arguments:
- pooled: bfloat16 [8, 3072, 1152], P('dp', 'fsdp'), may hold values from -6 to 6
- ln_gain: float32 [1152], replicated, may hold values from 0.5 to 1.5
- w_in: bfloat16 [1152, 4304], P('fsdp', 'tensor'), may hold values from -0.1875 to 0.1875
- w_out: bfloat16 [4304, 1152], P('tensor', 'fsdp'), may hold values from -0.09375 to 0.09375
- texts: bfloat16 [8, 3072, 1152], P('dp', ('fsdp', 'tensor')), may hold values from -6 to 6
Outputs:
- grad_pooled: float32 [8, 3072, 1152], P('dp', 'fsdp')
- grad_in: float32 [1152, 4304], P('fsdp', 'tensor')
- grad_out: float32 [4304, 1152], P('tensor', 'fsdp')
All inputs are finite; a program needn't handle non-finite values.
Results may differ from a plain program's by a relative error of at most 0.022.
Values may be sent and summed in bfloat16 or wider, within the bound.
A program may use at most 64 MiB of HBM per device.

v0:
```python
import jax
import jax.numpy as jnp
from jax import lax
from jax.sharding import PartitionSpec as P

ln_eps = 1e-06
norm_eps = 1e-06
logit_scale = 10.0
logit_bias = -2.0


def passed_along(block, axis, distance):
    devices = range(lax.axis_size(axis))
    route = [((i - distance) % len(devices), i) for i in devices]
    return lax.ppermute(block, axis, route)


def gelu_tanh(values):
    return jax.nn.gelu(values, approximate=True)


def unit_rows(values):
    return values / jnp.sqrt(jnp.sum(values * values, axis=-1, keepdims=True) + norm_eps)


def text_columns(first, number, block_rows, offset, stride):
    places = first + jnp.arange(number, dtype=jnp.int32)
    return places // block_rows * stride + offset + places % block_rows


def body(pooled, ln_gain, w_in, w_out, texts):
    rows = pooled[0].astype(jnp.float32)
    images = rows.shape[0]
    width = rows.shape[1]
    row_mean = jnp.mean(rows, axis=1, keepdims=True)
    centred = rows - row_mean
    inv_std = lax.rsqrt(jnp.mean(centred * centred, axis=1, keepdims=True) + ln_eps)
    normal_rows = centred * inv_std
    unit_in = (normal_rows * ln_gain).astype(jnp.bfloat16)
    full_in = lax.all_gather(w_in, "fsdp", axis=0, tiled=True)
    pre_act = jnp.dot(unit_in, full_in, preferred_element_type=jnp.float32)
    hidden = gelu_tanh(pre_act).astype(jnp.bfloat16)
    full_out = lax.all_gather(w_out, "fsdp", axis=1, tiled=True)
    partial_mix = jnp.dot(hidden, full_out, preferred_element_type=jnp.float32)
    mixed = rows + lax.psum(partial_mix.astype(jnp.bfloat16), "tensor").astype(jnp.float32)
    row_norm = jnp.sqrt(jnp.sum(mixed * mixed, axis=1, keepdims=True) + norm_eps)
    image_unit = mixed / row_norm
    image_b = image_unit.astype(jnp.bfloat16)
    text_b = unit_rows(texts[0].astype(jnp.float32)).astype(jnp.bfloat16)
    cycle_index = lax.axis_index("fsdp")
    cycle_size = lax.axis_size("fsdp")
    image_places = cycle_index * images + jnp.arange(images, dtype=jnp.int32)
    offset = lax.axis_index("tensor") * text_b.shape[0]
    block_rows = text_b.shape[0]

    def score_block(running, block, columns):
        logits = (
            logit_scale
            * jnp.einsum("rd,cd->rc", image_b, block, preferred_element_type=jnp.float32)
            + logit_bias
        )
        match = (image_places[:, None] == columns[None, :]).astype(jnp.float32)
        weights = (jax.nn.sigmoid(logits) - match).astype(jnp.bfloat16)
        return running + jnp.dot(weights, block, preferred_element_type=jnp.float32)

    def source_columns(source):
        return text_columns(source * block_rows, block_rows, block_rows, offset, images)

    empty = jnp.zeros((images, width), jnp.float32)
    running = score_block(empty, text_b, source_columns(cycle_index))

    def cycle_turn(turn, carry):
        total, moving = carry
        moving = passed_along(moving, "fsdp", 1)
        total = score_block(total, moving, source_columns((cycle_index - turn) % cycle_size))
        return (total, moving)

    running, _ = lax.fori_loop(1, cycle_size, cycle_turn, (running, text_b))
    grad_unit = logit_scale * running
    grad_unit = lax.psum(grad_unit.astype(jnp.bfloat16), "tensor").astype(jnp.float32)
    grad_mixed = (
        grad_unit - image_unit * jnp.sum(image_unit * grad_unit, axis=1, keepdims=True)
    ) / row_norm
    grad_b = grad_mixed.astype(jnp.bfloat16)
    grad_hidden = jnp.einsum("rd,fd->rf", grad_b, full_out, preferred_element_type=jnp.float32)
    _, gelu_back = jax.vjp(gelu_tanh, pre_act)
    grad_pre = gelu_back(grad_hidden)[0].astype(jnp.bfloat16)
    partial_unit = jnp.einsum("rf,df->rd", grad_pre, full_in, preferred_element_type=jnp.float32)
    grad_unit_in = lax.psum(partial_unit.astype(jnp.bfloat16), "tensor").astype(jnp.float32)
    scaled = grad_unit_in * ln_gain
    grad_rows = inv_std * (
        scaled
        - jnp.mean(scaled, axis=1, keepdims=True)
        - normal_rows * jnp.mean(scaled * normal_rows, axis=1, keepdims=True)
    )
    grad_pooled = (grad_mixed + grad_rows)[None]
    grad_in_part = lax.psum_scatter(
        jnp.einsum("rd,rf->df", unit_in, grad_pre, preferred_element_type=jnp.float32).astype(
            jnp.bfloat16
        ),
        "fsdp",
        scatter_dimension=0,
        tiled=True,
    )
    out_term = jnp.einsum("rf,rd->fd", hidden, grad_b, preferred_element_type=jnp.float32)
    grad_out_part = lax.psum_scatter(
        out_term.astype(jnp.bfloat16), "fsdp", scatter_dimension=1, tiled=True
    )
    grad_in, grad_out = (
        lax.psum(grad_in_part, "dp").astype(jnp.float32),
        lax.psum(grad_out_part, "dp").astype(jnp.float32),
    )
    return (grad_pooled, grad_in, grad_out)


def solution(mesh):
    placed = (
        P("dp", "fsdp", None),
        P(),
        P("fsdp", "tensor"),
        P("tensor", "fsdp"),
        P("dp", ("fsdp", "tensor"), None),
    )
    return jax.shard_map(
        body,
        mesh=mesh,
        in_specs=placed,
        out_specs=(P("dp", "fsdp", None), P("fsdp", "tensor"), P("tensor", "fsdp")),
        check_vma=False,
    )
```

profile of v0, /device:TPU:32, one launch (start us, length us, event | category | flops | bytes accessed | tf_op | source)
XLA Modules:
  0.0 573.5 jit_solution(10789957357336990693)
XLA Ops:
  12.3 42.3 %all-gather.3.cloned.1.call-done = bf16[1152,2152]{1,0:T(8,128)(2,1)} async-done(((bf16[72,2152]{1,0:T(8,128)(2,1)}), bf16[1152,2152]{1,0:T(8,128)(2,1)}) %all-gather.3.cloned.1.call-update) | async-done | bytes 4958224 | tf_op jit(solution)/shard_map/all_gather | solution.py:40
  54.6 3.8 fusion.72
  58.5 39.3 %all-gather.5.cloned.1.call-done = bf16[2152,1152]{0,1:T(8,128)(2,1)} async-done(((bf16[2152,72]{0,1:T(8,128)(2,1)}), bf16[2152,1152]{0,1:T(8,128)(2,1)}) %all-gather.5.cloned.1.call-update) | async-done | bytes 4958224 | tf_op jit(solution)/shard_map/all_gather | solution.py:43
  97.7 4.9 convolution_convert_fusion.3
  102.8 39.1 %all-reduce.8.cloned.1.call-done = bf16[192,1152]{1,0:T(8,128)(2,1)} async-done(((bf16[192,1152]{1,0:T(8,128)(2,1)}), bf16[192,1152]{1,0:T(8,128)(2,1)}) %all-reduce.8.cloned.1.call-update) | async-done | bytes 442384 | tf_op jit(solution)/shard_map/psum | solution.py:45
  145.0 101.4 %while.19 = (s32[]{:T(128)}, f32[192,1152]{1,0:T(8,128)S(1)}, bf16[96,1152]{1,0:T(8,128)(2,1)S(1)}, bf16[192,1152]{1,0:T(8,128)(2,1)S(1)}, s32[]{:T(128)}, /*ind...) while((s32[]{:T(128)}, f32[192,1152]{1,0:T(8,128)S(1)}, ...), condition=%wide.region_6.7_spmd.clone, body=%wide.region_5.6_spmd.clone.sunk | while | flops 85323472 | bytes 3762734 | solution.py:78
  145.1 5.3 collective-permute-done
  151.2 5.3 collective-permute-done
  157.3 5.3 collective-permute-done
  163.4 5.3 collective-permute-done
  169.4 5.3 collective-permute-done
  175.5 5.3 collective-permute-done
  181.6 5.8 %collective-permute-done = bf16[96,1152]{1,0:T(8,128)(2,1)S(1)} collective-permute-done((bf16[96,1152]{1,0:T(8,128)(2,1)S(1)}, bf16[96,1152]{1,0:T(8,128)(2,1)S(1)}, u32[]{:S(2)}, u32[]{:S(2)}) %collective-permute-start) | collective-permute-done | bytes 221216 | tf_op jit(solution)/shard_map/while/body/eval_jaxpr/ppermute | solution.py:15
  188.2 6.5 %collective-permute-done = bf16[96,1152]{1,0:T(8,128)(2,1)S(1)} collective-permute-done((bf16[96,1152]{1,0:T(8,128)(2,1)S(1)}, bf16[96,1152]{1,0:T(8,128)(2,1)S(1)}, u32[]{:S(2)}, u32[]{:S(2)}) %collective-permute-start) | collective-permute-done | bytes 221216 | tf_op jit(solution)/shard_map/while/body/eval_jaxpr/ppermute | solution.py:15
  195.5 6.5 %collective-permute-done = bf16[96,1152]{1,0:T(8,128)(2,1)S(1)} collective-permute-done((bf16[96,1152]{1,0:T(8,128)(2,1)S(1)}, bf16[96,1152]{1,0:T(8,128)(2,1)S(1)}, u32[]{:S(2)}, u32[]{:S(2)}) %collective-permute-start) | collective-permute-done | bytes 221216 | tf_op jit(solution)/shard_map/while/body/eval_jaxpr/ppermute | solution.py:15
  202.8 6.5 %collective-permute-done = bf16[96,1152]{1,0:T(8,128)(2,1)S(1)} collective-permute-done((bf16[96,1152]{1,0:T(8,128)(2,1)S(1)}, bf16[96,1152]{1,0:T(8,128)(2,1)S(1)}, u32[]{:S(2)}, u32[]{:S(2)}) %collective-permute-start) | collective-permute-done | bytes 221216 | tf_op jit(solution)/shard_map/while/body/eval_jaxpr/ppermute | solution.py:15
  210.1 6.5 %collective-permute-done = bf16[96,1152]{1,0:T(8,128)(2,1)S(1)} collective-permute-done((bf16[96,1152]{1,0:T(8,128)(2,1)S(1)}, bf16[96,1152]{1,0:T(8,128)(2,1)S(1)}, u32[]{:S(2)}, u32[]{:S(2)}) %collective-permute-start) | collective-permute-done | bytes 221216 | tf_op jit(solution)/shard_map/while/body/eval_jaxpr/ppermute | solution.py:15
  217.4 6.5 %collective-permute-done = bf16[96,1152]{1,0:T(8,128)(2,1)S(1)} collective-permute-done((bf16[96,1152]{1,0:T(8,128)(2,1)S(1)}, bf16[96,1152]{1,0:T(8,128)(2,1)S(1)}, u32[]{:S(2)}, u32[]{:S(2)}) %collective-permute-start) | collective-permute-done | bytes 221216 | tf_op jit(solution)/shard_map/while/body/eval_jaxpr/ppermute | solution.py:15
  224.7 6.5 %collective-permute-done = bf16[96,1152]{1,0:T(8,128)(2,1)S(1)} collective-permute-done((bf16[96,1152]{1,0:T(8,128)(2,1)S(1)}, bf16[96,1152]{1,0:T(8,128)(2,1)S(1)}, u32[]{:S(2)}, u32[]{:S(2)}) %collective-permute-start) | collective-permute-done | bytes 221216 | tf_op jit(solution)/shard_map/while/body/eval_jaxpr/ppermute | solution.py:15
  232.0 6.5 %collective-permute-done = bf16[96,1152]{1,0:T(8,128)(2,1)S(1)} collective-permute-done((bf16[96,1152]{1,0:T(8,128)(2,1)S(1)}, bf16[96,1152]{1,0:T(8,128)(2,1)S(1)}, u32[]{:S(2)}, u32[]{:S(2)}) %collective-permute-start) | collective-permute-done | bytes 221216 | tf_op jit(solution)/shard_map/while/body/eval_jaxpr/ppermute | solution.py:15
  239.3 6.5 %collective-permute-done = bf16[96,1152]{1,0:T(8,128)(2,1)S(1)} collective-permute-done((bf16[96,1152]{1,0:T(8,128)(2,1)S(1)}, bf16[96,1152]{1,0:T(8,128)(2,1)S(1)}, u32[]{:S(2)}, u32[]{:S(2)}) %collective-permute-start) | collective-permute-done | bytes 221216 | tf_op jit(solution)/shard_map/while/body/eval_jaxpr/ppermute | solution.py:15
  247.4 47.6 %all-reduce.10.cloned.1.call-done = bf16[192,1152]{1,0:T(8,128)(2,1)} async-done(((bf16[192,1152]{1,0:T(8,128)(2,1)}), bf16[192,1152]{1,0:T(8,128)(2,1)}) %all-reduce.10.cloned.1.call-update) | async-done | bytes 442384 | tf_op jit(solution)/shard_map/psum | solution.py:80
  296.4 4.7 fusion.26
  301.2 2.4 convolution_convert_fusion.2
  303.7 3.9 convolution_convert_fusion.1
  308.6 4.1 convolution_convert_fusion
  312.8 30.4 %all-reduce.12.cloned.1.call-done = bf16[192,1152]{1,0:T(8,128)(2,1)} async-done(((bf16[192,1152]{1,0:T(8,128)(2,1)}), bf16[192,1152]{1,0:T(8,128)(2,1)}) %all-reduce.12.cloned.1.call-update) | async-done | bytes 442384 | tf_op jit(solution)/shard_map/psum | solution.py:89
  344.7 64.2 %reduce-scatter.7.cloned.1.call-done = bf16[72,2152]{1,0:T(8,128)(2,1)} async-done(((bf16[1152,2152]{1,0:T(8,128)(2,1)}), bf16[72,2152]{1,0:T(8,128)(2,1)}) %reduce-scatter.7.cloned.1.call-update) | async-done | bytes 309904
  408.9 68.5 %reduce-scatter.9.cloned.1.call-done = bf16[2152,72]{0,1:T(8,128)(2,1)} async-done(((bf16[2152,1152]{0,1:T(8,128)(2,1)}), bf16[2152,72]{0,1:T(8,128)(2,1)}) %reduce-scatter.9.cloned.1.call-update) | async-done | bytes 309904
  478.9 84.1 %all-reduce.14.cloned.1.call-done = (bf16[72,2152]{1,0:T(8,128)(2,1)}, bf16[2152,72]{0,1:T(8,128)(2,1)}) async-done(((bf16[72,2152]{1,0:T(8,128)(2,1)}, bf16[2152,72]{0,1:T(8,128)(2,1)}), (bf16[72,2152]{1,0:T(8,128)(2,1)}, bf16[2152,72]{0,1:T(8,128)(2,1)})) %all-reduce.14.cloned.1.call-update) | async-done | bytes 619792 | tf_op jit(solution)/shard_map/psum | solution.py:110
  563.0 1.8 convert_element_type.107
  564.9 1.8 convert_element_type.109
  (130 shorter events, 25.7 us)
Async XLA Ops:
  7.2 47.5 %copy-start = (bf16[1,192,1152]{2,1,0:T(8,128)(2,1)S(1)}, bf16[1,192,1152]{2,1,0:T(8,128)(2,1)}, u32[]{:S(2)}) copy-start(bf16[1,192,1152]{2,1,0:T(8,128)(2,1)} %param.7) | copy-start | bytes 1327108
  7.2 47.5 %copy-start.7 = (f32[1152]{0:T(1024)S(1)}, f32[1152]{0:T(1024)}, u32[]{:S(2)}) copy-start(f32[1152]{0:T(1024)} %param.8) | copy-start | bytes 13828
  7.2 47.4 %all-gather.3.cloned.1.call-start = ((), (), s32[]{:S(2)}) async-start(), calls=%async_computation.2 | async-start | bytes 5326848 | tf_op jit(solution)/shard_map/all_gather | solution.py:40
  7.9 89.8 %all-gather.5.cloned.1.call-start = ((), (), s32[]{:S(2)}) async-start(), calls=%async_computation.3 | async-start | bytes 5326848 | tf_op jit(solution)/shard_map/all_gather | solution.py:43
  8.7 133.3 %all-reduce.8.cloned.1.call-start = ((), (), s32[]{:S(2)}) async-start(), calls=%async_computation.4 | async-start | bytes 884736 | tf_op jit(solution)/shard_map/psum | solution.py:45
  58.4 44.2 %copy-start.4 = (f32[192,2152]{1,0:T(8,128)}, f32[192,2152]{1,0:T(8,128)S(1)}, u32[]{:S(2)}) copy-start(f32[192,2152]{1,0:T(8,128)S(1)} %fusion.72) | copy-start | bytes 4958212
  58.5 44.2 %copy-start.6 = (bf16[1,96,1152]{2,1,0:T(8,128)(2,1)S(1)}, bf16[1,96,1152]{2,1,0:T(8,128)(2,1)}, u32[]{:S(2)}) copy-start(bf16[1,96,1152]{2,1,0:T(8,128)(2,1)} %param.11) | copy-start | bytes 663556
  102.6 192.3 %all-reduce.10.cloned.1.call-start = ((), (), s32[]{:S(2)}) async-start(), calls=%async_computation.5 | async-start | bytes 884736 | tf_op jit(solution)/shard_map/psum | solution.py:80
  145.0 5.4 collective-permute-start
  151.1 5.4 collective-permute-start
  157.2 5.4 collective-permute-start
  163.3 5.4 collective-permute-start
  169.4 5.4 collective-permute-start
  175.4 5.4 collective-permute-start
  181.5 5.9 %collective-permute-start = (bf16[96,1152]{1,0:T(8,128)(2,1)S(1)}, bf16[96,1152]{1,0:T(8,128)(2,1)S(1)}, u32[]{:S(2)}, u32[]{:S(2)}) collective-permute-start(bf16[96,1152]{1,0:T(8,128)(2,1)S(1)} %get-tuple-element.306), channel_id=1, source_target_pairs={{30,0},{0,2},{2,4},{4,6},{6,8},{8,10},{10,12},{12,14},{14,16},{16,... | collective-permute-start | bytes 663560 | tf_op jit(solution)/shard_map/while/body/eval_jaxpr/ppermute | solution.py:15
  188.1 6.6 %collective-permute-start = (bf16[96,1152]{1,0:T(8,128)(2,1)S(1)}, bf16[96,1152]{1,0:T(8,128)(2,1)S(1)}, u32[]{:S(2)}, u32[]{:S(2)}) collective-permute-start(bf16[96,1152]{1,0:T(8,128)(2,1)S(1)} %get-tuple-element.306), channel_id=1, source_target_pairs={{30,0},{0,2},{2,4},{4,6},{6,8},{8,10},{10,12},{12,14},{14,16},{16,... | collective-permute-start | bytes 663560 | tf_op jit(solution)/shard_map/while/body/eval_jaxpr/ppermute | solution.py:15
  195.4 6.6 %collective-permute-start = (bf16[96,1152]{1,0:T(8,128)(2,1)S(1)}, bf16[96,1152]{1,0:T(8,128)(2,1)S(1)}, u32[]{:S(2)}, u32[]{:S(2)}) collective-permute-start(bf16[96,1152]{1,0:T(8,128)(2,1)S(1)} %get-tuple-element.306), channel_id=1, source_target_pairs={{30,0},{0,2},{2,4},{4,6},{6,8},{8,10},{10,12},{12,14},{14,16},{16,... | collective-permute-start | bytes 663560 | tf_op jit(solution)/shard_map/while/body/eval_jaxpr/ppermute | solution.py:15
  202.7 6.6 %collective-permute-start = (bf16[96,1152]{1,0:T(8,128)(2,1)S(1)}, bf16[96,1152]{1,0:T(8,128)(2,1)S(1)}, u32[]{:S(2)}, u32[]{:S(2)}) collective-permute-start(bf16[96,1152]{1,0:T(8,128)(2,1)S(1)} %get-tuple-element.306), channel_id=1, source_target_pairs={{30,0},{0,2},{2,4},{4,6},{6,8},{8,10},{10,12},{12,14},{14,16},{16,... | collective-permute-start | bytes 663560 | tf_op jit(solution)/shard_map/while/body/eval_jaxpr/ppermute | solution.py:15
  210.0 6.6 %collective-permute-start = (bf16[96,1152]{1,0:T(8,128)(2,1)S(1)}, bf16[96,1152]{1,0:T(8,128)(2,1)S(1)}, u32[]{:S(2)}, u32[]{:S(2)}) collective-permute-start(bf16[96,1152]{1,0:T(8,128)(2,1)S(1)} %get-tuple-element.306), channel_id=1, source_target_pairs={{30,0},{0,2},{2,4},{4,6},{6,8},{8,10},{10,12},{12,14},{14,16},{16,... | collective-permute-start | bytes 663560 | tf_op jit(solution)/shard_map/while/body/eval_jaxpr/ppermute | solution.py:15
  217.3 6.6 %collective-permute-start = (bf16[96,1152]{1,0:T(8,128)(2,1)S(1)}, bf16[96,1152]{1,0:T(8,128)(2,1)S(1)}, u32[]{:S(2)}, u32[]{:S(2)}) collective-permute-start(bf16[96,1152]{1,0:T(8,128)(2,1)S(1)} %get-tuple-element.306), channel_id=1, source_target_pairs={{30,0},{0,2},{2,4},{4,6},{6,8},{8,10},{10,12},{12,14},{14,16},{16,... | collective-permute-start | bytes 663560 | tf_op jit(solution)/shard_map/while/body/eval_jaxpr/ppermute | solution.py:15
  224.6 6.6 %collective-permute-start = (bf16[96,1152]{1,0:T(8,128)(2,1)S(1)}, bf16[96,1152]{1,0:T(8,128)(2,1)S(1)}, u32[]{:S(2)}, u32[]{:S(2)}) collective-permute-start(bf16[96,1152]{1,0:T(8,128)(2,1)S(1)} %get-tuple-element.306), channel_id=1, source_target_pairs={{30,0},{0,2},{2,4},{4,6},{6,8},{8,10},{10,12},{12,14},{14,16},{16,... | collective-permute-start | bytes 663560 | tf_op jit(solution)/shard_map/while/body/eval_jaxpr/ppermute | solution.py:15
  231.9 6.6 %collective-permute-start = (bf16[96,1152]{1,0:T(8,128)(2,1)S(1)}, bf16[96,1152]{1,0:T(8,128)(2,1)S(1)}, u32[]{:S(2)}, u32[]{:S(2)}) collective-permute-start(bf16[96,1152]{1,0:T(8,128)(2,1)S(1)} %get-tuple-element.306), channel_id=1, source_target_pairs={{30,0},{0,2},{2,4},{4,6},{6,8},{8,10},{10,12},{12,14},{14,16},{16,... | collective-permute-start | bytes 663560 | tf_op jit(solution)/shard_map/while/body/eval_jaxpr/ppermute | solution.py:15
  239.2 6.6 %collective-permute-start = (bf16[96,1152]{1,0:T(8,128)(2,1)S(1)}, bf16[96,1152]{1,0:T(8,128)(2,1)S(1)}, u32[]{:S(2)}, u32[]{:S(2)}) collective-permute-start(bf16[96,1152]{1,0:T(8,128)(2,1)S(1)} %get-tuple-element.306), channel_id=1, source_target_pairs={{30,0},{0,2},{2,4},{4,6},{6,8},{8,10},{10,12},{12,14},{14,16},{16,... | collective-permute-start | bytes 663560 | tf_op jit(solution)/shard_map/while/body/eval_jaxpr/ppermute | solution.py:15
  246.5 48.5 %copy-start.1 = (bf16[192,1152]{1,0:T(8,128)(2,1)S(1)}, bf16[192,1152]{1,0:T(8,128)(2,1)}, u32[]{:S(2)}) copy-start(bf16[192,1152]{1,0:T(8,128)(2,1)} %all-reduce.8.cloned.1.call-done) | copy-start | bytes 1327108
  246.5 49.9 %copy-start.5 = (f32[192,2152]{1,0:T(8,128)S(1)}, f32[192,2152]{1,0:T(8,128)}, u32[]{:S(2)}) copy-start(f32[192,2152]{1,0:T(8,128)} %copy-done.4) | copy-start | bytes 4958212
  247.3 95.9 %all-reduce.12.cloned.1.call-start = ((), (), s32[]{:S(2)}) async-start(), calls=%async_computation.6 | async-start | bytes 884736 | tf_op jit(solution)/shard_map/psum | solution.py:89
  294.9 6.2 %slice-start = ((s8[5013504]{0:T(1024)(128)(4,1)}), s8[4194304]{0:T(1024)(128)(4,1)S(1)}, s32[]{:S(2)}) async-start(s8[5013504]{0:T(1024)(128)(4,1)} %bitcast.75), calls=%async_computation.10 | async-start | bytes 8388608
  296.4 4.8 slice-start.1
  303.6 105.3 %reduce-scatter.7.cloned.1.call-start = ((), (), s32[]{:S(2)}) async-start(), calls=%async_computation.7 | async-start | bytes 5326848
  307.6 169.8 %reduce-scatter.9.cloned.1.call-start = ((), (), s32[]{:S(2)}) async-start(), calls=%async_computation.8 | async-start | bytes 5326848
  312.8 250.3 %all-reduce.14.cloned.1.call-start = ((), (), s32[]{:S(2)}) async-start(), calls=%async_computation.9 | async-start | bytes 1253376 | tf_op jit(solution)/shard_map/psum | solution.py:110
  343.3 134.2 %copy-start.2 = (bf16[192,1152]{1,0:T(8,128)(2,1)S(1)}, bf16[192,1152]{1,0:T(8,128)(2,1)}, u32[]{:S(2)}) copy-start(bf16[192,1152]{1,0:T(8,128)(2,1)} %all-reduce.12.cloned.1.call-done) | copy-start | bytes 1327108
  (1 other events, 1.0 us)
Sparse Core Ops, SparseCore 0:
  9.8 44.7 all-gather.2
  56.5 41.2 all-gather.4
  102.8 39.1 all-reduce.7
  247.4 47.4 all-reduce.9
  303.7 39.4 all-reduce.11
  345.7 63.1 reduce-scatter.6
  411.5 65.8 reduce-scatter.8
  480.1 82.8 all-reduce.13
where the time goes:
time: 574 us
  waiting for transfers between devices  507 us (88%)
  matrix products  34.6 us (6%)
  other arithmetic  15.3 us (3%)
  between operations  14.3 us (2%)
    unnamed x10, waiting for transfers between devices  134 us
    ppermute x15, waiting for transfers between devices, passed_along(): return lax.ppermute(block, axis, route)  89.5 us
    psum x1, waiting for transfers between devices, body(): lax.psum(grad_in_part, 'dp').astype(jnp.float32)  84.1 us
    psum x1, waiting for transfers between devices, body(): lax.psum(grad_unit.astype(jnp.bfloat16), 'tensor').astype(jnp.float32)  47.6 us
    all_gather x1, waiting for transfers between devices, body(): full_in = lax.all_gather(w_in, 'fsdp', axis=0, tiled=True)  42.3 us
    all_gather x1, waiting for transfers between devices, body(): full_out = lax.all_gather(w_out, 'fsdp', axis=1, tiled=True)  39.3 us
    psum x1, waiting for transfers between devices, body(): lax.psum(partial_mix.astype(jnp.bfloat16), 'tensor').astype(jnp.float32)  39.1 us
    psum x1, waiting for transfers between devices, body(): lax.psum(partial_unit.astype(jnp.bfloat16), 'tensor').astype(jnp.float32)  30.4 us
  transfers between devices with their start and end apart: 23, of which 23 were waited for; matrix products, arithmetic and copies ran while one was open for 3% of the time, Pallas kernels for 0%

commit v1 on v0

--- a/solution.py
+++ b/solution.py
@@ -37,7 +37,16 @@
     inv_std = lax.rsqrt(jnp.mean(centred * centred, axis=1, keepdims=True) + ln_eps)
     normal_rows = centred * inv_std
     unit_in = (normal_rows * ln_gain).astype(jnp.bfloat16)
-    full_in = lax.all_gather(w_in, "fsdp", axis=0, tiled=True)
+    hubs_drive = lambda row_data, a_name, pos_dim: jnp.concatenate(
+        lax.all_to_all(
+            jnp.stack([row_data for _ in range(lax.psum(1, axis_name=a_name))]),
+            a_name,
+            split_axis=0,
+            concat_axis=0,
+        ),
+        axis=pos_dim,
+    )
+    full_in = hubs_drive(w_in, "fsdp", 0)
     pre_act = jnp.dot(unit_in, full_in, preferred_element_type=jnp.float32)
     hidden = gelu_tanh(pre_act).astype(jnp.bfloat16)
     full_out = lax.all_gather(w_out, "fsdp", axis=1, tiled=True)

time: 574 us -> 637 us (1.11)
  waiting for transfers between devices: 507 us -> 558 us
  starting transfers between devices: 0.78 us -> 9.46 us
    all_to_all x0 -> x1, waiting for transfers between devices: none -> 132 us  [body(): lax.all_to_all(jnp.stack([row_data for _ in range(lax.psum(1, axis_name=a...]
    all_gather x1 -> x0, waiting for transfers between devices: 42.3 us -> none  [body(): full_in = lax.all_gather(w_in, 'fsdp', axis=0, tiled=True)]
    all_gather x1, waiting for transfers between devices: 39.3 us -> 0.02 us  [body(): full_out = lax.all_gather(w_out, 'fsdp', axis=1, tiled=True)]
    all_to_all x0 -> x1, starting transfers between devices: none -> 8.72 us  [body(): lax.all_to_all(jnp.stack([row_data for _ in range(lax.psum(1, axis_name=a...]
    unnamed x10 -> x9, waiting for transfers between devices: 134 us -> 133 us
  transfers between devices with their start and end apart: 23 -> 23, of which waited for: 23 -> 22; matrix products, arithmetic and copies ran while one was open for 3% -> 2% of each run, Pallas kernels for 0% -> 0%
where the time goes in v1:
time: 637 us
  waiting for transfers between devices  558 us (88%)
  matrix products  37.5 us (6%)
  between operations  14.3 us (2%)
  other arithmetic  12.2 us (2%)
  starting transfers between devices  9.46 us (1%)
    unnamed x9, waiting for transfers between devices  133 us
    all_to_all x1, waiting for transfers between devices, body(): lax.all_to_all(jnp.stack([row_data for _ in range(lax.psum(1, axis_name=a...  132 us
    ppermute x15, waiting for transfers between devices, passed_along(): return lax.ppermute(block, axis, route)  89.5 us
    psum x1, waiting for transfers between devices, body(): lax.psum(grad_in_part, 'dp').astype(jnp.float32)  84.1 us
    psum x1, waiting for transfers between devices, body(): lax.psum(grad_unit.astype(jnp.bfloat16), 'tensor').astype(jnp.float32)  47.6 us
    psum x1, waiting for transfers between devices, body(): lax.psum(partial_mix.astype(jnp.bfloat16), 'tensor').astype(jnp.float32)  40.9 us
    psum x1, waiting for transfers between devices, body(): lax.psum(partial_unit.astype(jnp.bfloat16), 'tensor').astype(jnp.float32)  30.4 us
  transfers between devices with their start and end apart: 23, of which 22 were waited for; matrix products, arithmetic and copies ran while one was open for 2% of the time, Pallas kernels for 0%

profile of v1, /device:TPU:32, one launch (start us, length us, event | category | flops | bytes accessed | tf_op | source)
XLA Modules:
  0.0 636.8 jit_solution(16381642714148368896)
XLA Ops:
  7.2 3.6 stack.2
  10.8 8.7 %all-to-all-start = ((bf16[16,72,2152]{2,1,0:T(8,128)(2,1)}), bf16[16,72,2152]{2,1,0:T(8,128)(2,1)}, u32[]{:S(2)}, u32[]{:S(2)}) async-start(bf16[16,72,2152]{2,1,0:T(8,128)(2,1)} %stack.2), calls=%async_computation | async-start | bytes 10027008 | tf_op jit(solution)/shard_map/all_to_all | solution.py:41
  20.9 131.8 %all-to-all-done = bf16[16,72,2152]{2,1,0:T(8,128)(2,1)} async-done(((bf16[16,72,2152]{2,1,0:T(8,128)(2,1)}), bf16[16,72,2152]{2,1,0:T(8,128)(2,1)}, u32[]{:S(2)}, u32[]{:S(2)}) %all-to-all-start) | async-done | bytes 4958240 | tf_op jit(solution)/shard_map/all_to_all | solution.py:41
  152.8 3.8 fusion.59
  156.6 5.5 convolution_convert_fusion.3
  162.3 40.9 %all-reduce.8.cloned.1.call-done = bf16[192,1152]{1,0:T(8,128)(2,1)} async-done(((bf16[192,1152]{1,0:T(8,128)(2,1)}), bf16[192,1152]{1,0:T(8,128)(2,1)}) %all-reduce.8.cloned.1.call-update) | async-done | bytes 442384 | tf_op jit(solution)/shard_map/psum | solution.py:54
  206.3 101.4 %while.19 = (s32[]{:T(128)}, f32[192,1152]{1,0:T(8,128)S(1)}, bf16[96,1152]{1,0:T(8,128)(2,1)S(1)}, bf16[192,1152]{1,0:T(8,128)(2,1)S(1)}, s32[]{:T(128)}, /*ind...) while((s32[]{:T(128)}, f32[192,1152]{1,0:T(8,128)S(1)}, ...), condition=%wide.region_6.7_spmd.clone, body=%wide.region_5.6_spmd.clone.sunk | while | flops 85323472 | bytes 3762734 | solution.py:87
  206.4 5.3 collective-permute-done
  212.5 5.3 collective-permute-done
  218.5 5.3 collective-permute-done
  224.6 5.3 collective-permute-done
  230.7 5.3 collective-permute-done
  236.8 5.3 collective-permute-done
  242.9 5.8 collective-permute-done
  249.5 6.5 %collective-permute-done = bf16[96,1152]{1,0:T(8,128)(2,1)S(1)} collective-permute-done((bf16[96,1152]{1,0:T(8,128)(2,1)S(1)}, bf16[96,1152]{1,0:T(8,128)(2,1)S(1)}, u32[]{:S(2)}, u32[]{:S(2)}) %collective-permute-start) | collective-permute-done | bytes 221216 | tf_op jit(solution)/shard_map/while/body/eval_jaxpr/ppermute | solution.py:15
  256.8 6.5 %collective-permute-done = bf16[96,1152]{1,0:T(8,128)(2,1)S(1)} collective-permute-done((bf16[96,1152]{1,0:T(8,128)(2,1)S(1)}, bf16[96,1152]{1,0:T(8,128)(2,1)S(1)}, u32[]{:S(2)}, u32[]{:S(2)}) %collective-permute-start) | collective-permute-done | bytes 221216 | tf_op jit(solution)/shard_map/while/body/eval_jaxpr/ppermute | solution.py:15
  264.1 6.5 %collective-permute-done = bf16[96,1152]{1,0:T(8,128)(2,1)S(1)} collective-permute-done((bf16[96,1152]{1,0:T(8,128)(2,1)S(1)}, bf16[96,1152]{1,0:T(8,128)(2,1)S(1)}, u32[]{:S(2)}, u32[]{:S(2)}) %collective-permute-start) | collective-permute-done | bytes 221216 | tf_op jit(solution)/shard_map/while/body/eval_jaxpr/ppermute | solution.py:15
  271.3 6.5 %collective-permute-done = bf16[96,1152]{1,0:T(8,128)(2,1)S(1)} collective-permute-done((bf16[96,1152]{1,0:T(8,128)(2,1)S(1)}, bf16[96,1152]{1,0:T(8,128)(2,1)S(1)}, u32[]{:S(2)}, u32[]{:S(2)}) %collective-permute-start) | collective-permute-done | bytes 221216 | tf_op jit(solution)/shard_map/while/body/eval_jaxpr/ppermute | solution.py:15
  278.6 6.5 %collective-permute-done = bf16[96,1152]{1,0:T(8,128)(2,1)S(1)} collective-permute-done((bf16[96,1152]{1,0:T(8,128)(2,1)S(1)}, bf16[96,1152]{1,0:T(8,128)(2,1)S(1)}, u32[]{:S(2)}, u32[]{:S(2)}) %collective-permute-start) | collective-permute-done | bytes 221216 | tf_op jit(solution)/shard_map/while/body/eval_jaxpr/ppermute | solution.py:15
  285.9 6.5 %collective-permute-done = bf16[96,1152]{1,0:T(8,128)(2,1)S(1)} collective-permute-done((bf16[96,1152]{1,0:T(8,128)(2,1)S(1)}, bf16[96,1152]{1,0:T(8,128)(2,1)S(1)}, u32[]{:S(2)}, u32[]{:S(2)}) %collective-permute-start) | collective-permute-done | bytes 221216 | tf_op jit(solution)/shard_map/while/body/eval_jaxpr/ppermute | solution.py:15
  293.2 6.5 %collective-permute-done = bf16[96,1152]{1,0:T(8,128)(2,1)S(1)} collective-permute-done((bf16[96,1152]{1,0:T(8,128)(2,1)S(1)}, bf16[96,1152]{1,0:T(8,128)(2,1)S(1)}, u32[]{:S(2)}, u32[]{:S(2)}) %collective-permute-start) | collective-permute-done | bytes 221216 | tf_op jit(solution)/shard_map/while/body/eval_jaxpr/ppermute | solution.py:15
  300.5 6.5 %collective-permute-done = bf16[96,1152]{1,0:T(8,128)(2,1)S(1)} collective-permute-done((bf16[96,1152]{1,0:T(8,128)(2,1)S(1)}, bf16[96,1152]{1,0:T(8,128)(2,1)S(1)}, u32[]{:S(2)}, u32[]{:S(2)}) %collective-permute-start) | collective-permute-done | bytes 221216 | tf_op jit(solution)/shard_map/while/body/eval_jaxpr/ppermute | solution.py:15
  308.6 47.6 %all-reduce.10.cloned.1.call-done = bf16[192,1152]{1,0:T(8,128)(2,1)} async-done(((bf16[192,1152]{1,0:T(8,128)(2,1)}), bf16[192,1152]{1,0:T(8,128)(2,1)}) %all-reduce.10.cloned.1.call-update) | async-done | bytes 442384 | tf_op jit(solution)/shard_map/psum | solution.py:89
  357.5 4.7 fusion.26
  362.2 4.8 convolution_convert_fusion.2
  367.1 3.9 convolution_convert_fusion.1
  372.0 4.1 convolution_convert_fusion
  376.3 30.4 %all-reduce.12.cloned.1.call-done = bf16[192,1152]{1,0:T(8,128)(2,1)} async-done(((bf16[192,1152]{1,0:T(8,128)(2,1)}), bf16[192,1152]{1,0:T(8,128)(2,1)}) %all-reduce.12.cloned.1.call-update) | async-done | bytes 442384 | tf_op jit(solution)/shard_map/psum | solution.py:98
  408.1 64.2 %reduce-scatter.7.cloned.1.call-done = bf16[72,2152]{1,0:T(8,128)(2,1)} async-done(((bf16[1152,2152]{1,0:T(8,128)(2,1)}), bf16[72,2152]{1,0:T(8,128)(2,1)}) %reduce-scatter.7.cloned.1.call-update) | async-done | bytes 309904
  472.3 68.4 %reduce-scatter.9.cloned.1.call-done = bf16[2152,72]{0,1:T(8,128)(2,1)} async-done(((bf16[2152,1152]{0,1:T(8,128)(2,1)}), bf16[2152,72]{0,1:T(8,128)(2,1)}) %reduce-scatter.9.cloned.1.call-update) | async-done | bytes 309904
  542.2 84.1 %all-reduce.14.cloned.1.call-done = (bf16[72,2152]{1,0:T(8,128)(2,1)}, bf16[2152,72]{0,1:T(8,128)(2,1)}) async-done(((bf16[72,2152]{1,0:T(8,128)(2,1)}, bf16[2152,72]{0,1:T(8,128)(2,1)}), (bf16[72,2152]{1,0:T(8,128)(2,1)}, bf16[2152,72]{0,1:T(8,128)(2,1)})) %all-reduce.14.cloned.1.call-update) | async-done | bytes 619792 | tf_op jit(solution)/shard_map/psum | solution.py:119
  628.1 1.8 convert_element_type.117
  (125 shorter events, 23.7 us)
Async XLA Ops:
  10.8 9.5 %copy-start.6 = (bf16[1,96,1152]{2,1,0:T(8,128)(2,1)S(1)}, bf16[1,96,1152]{2,1,0:T(8,128)(2,1)}, u32[]{:S(2)}) copy-start(bf16[1,96,1152]{2,1,0:T(8,128)(2,1)} %param.11) | copy-start | bytes 663556
  10.8 9.7 %copy-start = (bf16[1,192,1152]{2,1,0:T(8,128)(2,1)S(1)}, bf16[1,192,1152]{2,1,0:T(8,128)(2,1)}, u32[]{:S(2)}) copy-start(bf16[1,192,1152]{2,1,0:T(8,128)(2,1)} %param.7) | copy-start | bytes 1327108
  10.8 142.0 %copy-start.7 = (f32[1152]{0:T(1024)S(1)}, f32[1152]{0:T(1024)}, u32[]{:S(2)}) copy-start(f32[1152]{0:T(1024)} %param.8) | copy-start | bytes 13828
  10.8 142.0 %all-to-all-start = ((bf16[16,72,2152]{2,1,0:T(8,128)(2,1)}), bf16[16,72,2152]{2,1,0:T(8,128)(2,1)}, u32[]{:S(2)}, u32[]{:S(2)}) async-start(bf16[16,72,2152]{2,1,0:T(8,128)(2,1)} %stack.2), calls=%async_computation | async-start | bytes 10027008 | tf_op jit(solution)/shard_map/all_to_all | solution.py:41
  19.5 137.1 %all-gather.2.cloned.1.call-start = ((), (), s32[]{:S(2)}) async-start(), calls=%async_computation.3 | async-start | bytes 5326848 | tf_op jit(solution)/shard_map/all_gather | solution.py:52
  20.3 182.9 %all-reduce.8.cloned.1.call-start = ((), (), s32[]{:S(2)}) async-start(), calls=%async_computation.4 | async-start | bytes 884736 | tf_op jit(solution)/shard_map/psum | solution.py:54
  156.6 5.5 copy-start.4
  162.1 194.1 %all-reduce.10.cloned.1.call-start = ((), (), s32[]{:S(2)}) async-start(), calls=%async_computation.5 | async-start | bytes 884736 | tf_op jit(solution)/shard_map/psum | solution.py:89
  206.3 5.4 collective-permute-start
  212.4 5.4 collective-permute-start
  218.5 5.4 collective-permute-start
  224.5 5.4 collective-permute-start
  230.6 5.4 collective-permute-start
  236.7 5.4 collective-permute-start
  242.8 5.9 collective-permute-start
  249.4 6.6 %collective-permute-start = (bf16[96,1152]{1,0:T(8,128)(2,1)S(1)}, bf16[96,1152]{1,0:T(8,128)(2,1)S(1)}, u32[]{:S(2)}, u32[]{:S(2)}) collective-permute-start(bf16[96,1152]{1,0:T(8,128)(2,1)S(1)} %get-tuple-element.306), channel_id=1, source_target_pairs={{30,0},{0,2},{2,4},{4,6},{6,8},{8,10},{10,12},{12,14},{14,16},{16,... | collective-permute-start | bytes 663560 | tf_op jit(solution)/shard_map/while/body/eval_jaxpr/ppermute | solution.py:15
  256.7 6.6 %collective-permute-start = (bf16[96,1152]{1,0:T(8,128)(2,1)S(1)}, bf16[96,1152]{1,0:T(8,128)(2,1)S(1)}, u32[]{:S(2)}, u32[]{:S(2)}) collective-permute-start(bf16[96,1152]{1,0:T(8,128)(2,1)S(1)} %get-tuple-element.306), channel_id=1, source_target_pairs={{30,0},{0,2},{2,4},{4,6},{6,8},{8,10},{10,12},{12,14},{14,16},{16,... | collective-permute-start | bytes 663560 | tf_op jit(solution)/shard_map/while/body/eval_jaxpr/ppermute | solution.py:15
  264.0 6.6 %collective-permute-start = (bf16[96,1152]{1,0:T(8,128)(2,1)S(1)}, bf16[96,1152]{1,0:T(8,128)(2,1)S(1)}, u32[]{:S(2)}, u32[]{:S(2)}) collective-permute-start(bf16[96,1152]{1,0:T(8,128)(2,1)S(1)} %get-tuple-element.306), channel_id=1, source_target_pairs={{30,0},{0,2},{2,4},{4,6},{6,8},{8,10},{10,12},{12,14},{14,16},{16,... | collective-permute-start | bytes 663560 | tf_op jit(solution)/shard_map/while/body/eval_jaxpr/ppermute | solution.py:15
  271.3 6.6 %collective-permute-start = (bf16[96,1152]{1,0:T(8,128)(2,1)S(1)}, bf16[96,1152]{1,0:T(8,128)(2,1)S(1)}, u32[]{:S(2)}, u32[]{:S(2)}) collective-permute-start(bf16[96,1152]{1,0:T(8,128)(2,1)S(1)} %get-tuple-element.306), channel_id=1, source_target_pairs={{30,0},{0,2},{2,4},{4,6},{6,8},{8,10},{10,12},{12,14},{14,16},{16,... | collective-permute-start | bytes 663560 | tf_op jit(solution)/shard_map/while/body/eval_jaxpr/ppermute | solution.py:15
  278.6 6.6 %collective-permute-start = (bf16[96,1152]{1,0:T(8,128)(2,1)S(1)}, bf16[96,1152]{1,0:T(8,128)(2,1)S(1)}, u32[]{:S(2)}, u32[]{:S(2)}) collective-permute-start(bf16[96,1152]{1,0:T(8,128)(2,1)S(1)} %get-tuple-element.306), channel_id=1, source_target_pairs={{30,0},{0,2},{2,4},{4,6},{6,8},{8,10},{10,12},{12,14},{14,16},{16,... | collective-permute-start | bytes 663560 | tf_op jit(solution)/shard_map/while/body/eval_jaxpr/ppermute | solution.py:15
  285.8 6.6 %collective-permute-start = (bf16[96,1152]{1,0:T(8,128)(2,1)S(1)}, bf16[96,1152]{1,0:T(8,128)(2,1)S(1)}, u32[]{:S(2)}, u32[]{:S(2)}) collective-permute-start(bf16[96,1152]{1,0:T(8,128)(2,1)S(1)} %get-tuple-element.306), channel_id=1, source_target_pairs={{30,0},{0,2},{2,4},{4,6},{6,8},{8,10},{10,12},{12,14},{14,16},{16,... | collective-permute-start | bytes 663560 | tf_op jit(solution)/shard_map/while/body/eval_jaxpr/ppermute | solution.py:15
  293.1 6.6 %collective-permute-start = (bf16[96,1152]{1,0:T(8,128)(2,1)S(1)}, bf16[96,1152]{1,0:T(8,128)(2,1)S(1)}, u32[]{:S(2)}, u32[]{:S(2)}) collective-permute-start(bf16[96,1152]{1,0:T(8,128)(2,1)S(1)} %get-tuple-element.306), channel_id=1, source_target_pairs={{30,0},{0,2},{2,4},{4,6},{6,8},{8,10},{10,12},{12,14},{14,16},{16,... | collective-permute-start | bytes 663560 | tf_op jit(solution)/shard_map/while/body/eval_jaxpr/ppermute | solution.py:15
  300.4 6.6 %collective-permute-start = (bf16[96,1152]{1,0:T(8,128)(2,1)S(1)}, bf16[96,1152]{1,0:T(8,128)(2,1)S(1)}, u32[]{:S(2)}, u32[]{:S(2)}) collective-permute-start(bf16[96,1152]{1,0:T(8,128)(2,1)S(1)} %get-tuple-element.306), channel_id=1, source_target_pairs={{30,0},{0,2},{2,4},{4,6},{6,8},{8,10},{10,12},{12,14},{14,16},{16,... | collective-permute-start | bytes 663560 | tf_op jit(solution)/shard_map/while/body/eval_jaxpr/ppermute | solution.py:15
  307.7 48.5 %copy-start.1 = (bf16[192,1152]{1,0:T(8,128)(2,1)S(1)}, bf16[192,1152]{1,0:T(8,128)(2,1)}, u32[]{:S(2)}) copy-start(bf16[192,1152]{1,0:T(8,128)(2,1)} %all-reduce.8.cloned.1.call-done) | copy-start | bytes 1327108
  307.7 49.8 %copy-start.5 = (f32[192,2152]{1,0:T(8,128)S(1)}, f32[192,2152]{1,0:T(8,128)}, u32[]{:S(2)}) copy-start(f32[192,2152]{1,0:T(8,128)} %copy-done.4) | copy-start | bytes 4958212
  308.6 98.1 %all-reduce.12.cloned.1.call-start = ((), (), s32[]{:S(2)}) async-start(), calls=%async_computation.6 | async-start | bytes 884736 | tf_op jit(solution)/shard_map/psum | solution.py:98
  367.0 105.3 %reduce-scatter.7.cloned.1.call-start = ((), (), s32[]{:S(2)}) async-start(), calls=%async_computation.7 | async-start | bytes 5326848
  371.0 1.0 copy-start.3
  371.0 169.6 %reduce-scatter.9.cloned.1.call-start = ((), (), s32[]{:S(2)}) async-start(), calls=%async_computation.8 | async-start | bytes 5326848
  376.2 250.1 %all-reduce.14.cloned.1.call-start = ((), (), s32[]{:S(2)}) async-start(), calls=%async_computation.9 | async-start | bytes 1253376 | tf_op jit(solution)/shard_map/psum | solution.py:119
  406.7 134.0 %copy-start.2 = (bf16[192,1152]{1,0:T(8,128)(2,1)S(1)}, bf16[192,1152]{1,0:T(8,128)(2,1)}, u32[]{:S(2)}) copy-start(bf16[192,1152]{1,0:T(8,128)(2,1)} %all-reduce.12.cloned.1.call-done) | copy-start | bytes 1327108
Sparse Core Ops, SparseCore 0:
  22.2 111.6 all-gather.1
  162.2 40.9 all-reduce.7
  308.7 47.4 all-reduce.9
  367.1 39.4 all-reduce.11
  409.1 63.1 reduce-scatter.6
  474.7 65.8 reduce-scatter.8
  543.4 82.8 all-reduce.13
